TPU v7x, 256 devices: a whole 4x4x8 slice. The times are simulated.
256 devices in a mesh: bx: 4 (over y_hi, core), by: 8 (over y_lo, x), bz: 8 (over z).
Axes of the slice: x: 4, y: 4 (y_hi: 2, y_lo: 2; y = y_hi * 2 + y_lo), z: 8, core: 2. Of those that a mesh axis runs over, the one named last changes fastest.
Arguments:
- space_factor: float32 [64, 8, 64, 1024], P(None, 'bx', 'by', 'bz'), may hold values from -6 to 6
- core_matrix: float32 [64, 64], replicated, may hold values from -0.1 to 3
- velocity_factor: float32 [64, 32768], P(None, ('bx', 'by')), may hold values from -30 to 30
Outputs:
- new_space: float32 [64, 8, 64, 1024], P(None, 'bx', 'by', 'bz')
- new_core: float32 [64, 64], replicated
- new_velocity: float32 [64, 32768], P(None, ('bx', 'by'))
All inputs are finite; a program needn't handle non-finite values.
Results may differ from a plain program's by a relative error of at most 0.0028.
Values sent between devices are 32-bit elements; how exact they have to be, the bound alone decides.
No kernel may reach another device: no remote copies, remote signals or barrier semaphores. Data moves between devices by JAX's collectives and lax.ppermute only.
A program may use at most 64 MiB of HBM per device.

v0:
```python
import jax
import jax.numpy as jnp
from jax import lax
from jax.sharding import PartitionSpec as P

VEL_N = 32
STEPS = 2


TIME_STEP = 0.1
RELAX_RATE = 1.0
SPEED_MAX = 3.0
HIGHEST = lax.Precision.HIGHEST


def shifted_2(block, axis, distance):
    devices = range(lax.axis_size(axis))
    route = [((i - distance) % len(devices), i) for i in devices]
    return lax.ppermute(block, axis, route)


def padded_2(array, sides, width):
    for axis, dim in sides:
        size, length = (lax.axis_size(axis), array.shape[dim])
        up = [(i, (i + 1) % size) for i in range(size)]
        down = [(j, i) for i, j in up]
        last = lax.slice_in_dim(array, length - width, length, axis=dim)
        leading = lax.slice_in_dim(array, 0, width, axis=dim)
        before = lax.ppermute(last, axis, up)
        after = lax.ppermute(leading, axis, down)
        array = jnp.concatenate([before, array, after], axis=dim)
    return array


def matmul_hi(left_mat, right_mat):
    return jnp.dot(left_mat, right_mat, precision=HIGHEST)


def apply_left(matrix, field):
    return jnp.einsum("lj,lxyz->jxyz", matrix, field, precision=HIGHEST)


def contract(left_field, right_field):
    return lax.dot_general(
        left_field, right_field, (((1, 2, 3), (1, 2, 3)), ((), ())), precision=HIGHEST
    )


def velocity_tables(start, row_count):
    row_ids = start + jnp.arange(row_count, dtype=jnp.int32)
    levels = jnp.stack(
        [row_ids // (VEL_N * VEL_N), row_ids // VEL_N % VEL_N, row_ids % VEL_N]
    ).astype(jnp.float32)
    speeds = SPEED_MAX * (2.0 * levels + 1.0 - VEL_N) / VEL_N
    line_speeds = SPEED_MAX * (2.0 * jnp.arange(VEL_N, dtype=jnp.float32) + 1.0 - VEL_N) / VEL_N
    norm_one = jnp.mean(jnp.exp(-0.5 * line_speeds * line_speeds))
    weight = jnp.exp(-0.5 * jnp.sum(speeds * speeds, axis=0)) / (norm_one * norm_one * norm_one)
    eq_modes = jnp.stack(
        [
            weight,
            weight * speeds[0],
            weight * speeds[1],
            weight * speeds[2],
            0.5 * weight * (speeds[0] * speeds[0] - 1.0),
            0.5 * weight * (speeds[1] * speeds[1] - 1.0),
            0.5 * weight * (speeds[2] * speeds[2] - 1.0),
            weight * speeds[0] * speeds[1],
            weight * speeds[0] * speeds[2],
            weight * speeds[1] * speeds[2],
        ]
    )
    moment_rows = jnp.concatenate([jnp.ones_like(speeds[:1]), speeds], axis=0)
    return (speeds, eq_modes, moment_rows)


def quadratic(density):
    return jnp.stack(
        [
            density[0],
            density[1],
            density[2],
            density[3],
            density[1] * density[1],
            density[2] * density[2],
            density[3] * density[3],
            density[1] * density[2],
            density[1] * density[3],
            density[2] * density[3],
        ]
    )


def solve_rows(chol_low, field):
    flat_rows = field.reshape(field.shape[0], -1)
    solved = jax.scipy.linalg.solve_triangular(chol_low, flat_rows, lower=True)
    return solved.reshape(field.shape)


def from_below(field, plane, dim_index):
    length = field.shape[dim_index + 1]
    inner = lax.slice_in_dim(field, 0, length - 1, axis=dim_index + 1)
    return jnp.concatenate([plane, inner], axis=dim_index + 1)


def from_above(field, plane, dim_index):
    length = field.shape[dim_index + 1]
    inner = lax.slice_in_dim(field, 1, length, axis=dim_index + 1)
    return jnp.concatenate([inner, plane], axis=dim_index + 1)


def lower_faces(field):
    from_x = shifted_2(field[:, -1:, :, :], "bx", 1)
    from_y = shifted_2(field[:, :, -1:, :], "by", 1)
    from_z = shifted_2(field[:, :, :, -1:], "bz", 1)
    return (from_x, from_y, from_z)


def full_rims(field):
    padded = padded_2(field, (("bx", 1), ("by", 2), ("bz", 3)), 1)
    low_faces = (padded[:, :1, 1:-1, 1:-1], padded[:, 1:-1, :1, 1:-1], padded[:, 1:-1, 1:-1, :1])
    up_faces = (padded[:, -1:, 1:-1, 1:-1], padded[:, 1:-1, -1:, 1:-1], padded[:, 1:-1, 1:-1, -1:])
    return (low_faces, up_faces)


def velocity_terms(v_rows, tables):
    speeds, eq_modes, moment_rows = tables
    plus_raw = jnp.einsum(
        "dkv,jv->dkj", v_rows[None] * jnp.maximum(speeds, 0.0)[:, None], v_rows, precision=HIGHEST
    )
    minus_raw = jnp.einsum(
        "dkv,jv->dkj", v_rows[None] * jnp.minimum(speeds, 0.0)[:, None], v_rows, precision=HIGHEST
    )
    return (plus_raw, minus_raw, matmul_hi(moment_rows, v_rows.T), matmul_hi(eq_modes, v_rows.T))


def plain_velocity(raw_rows, row_total):
    gram_mat = lax.psum(matmul_hi(raw_rows, raw_rows.T), ("bx", "by"))
    chol_low = jnp.linalg.cholesky(gram_mat / row_total)
    return (jax.scipy.linalg.solve_triangular(chol_low, raw_rows, lower=True), chol_low)


def orthonormal_velocity(raw_rows, tables, need_ops):
    row_total = VEL_N**3
    v_rows, chol_low = plain_velocity(raw_rows, row_total)
    if not need_ops:
        return (v_rows, chol_low, None)
    plus_raw, minus_raw, moment_raw, proj_raw = velocity_terms(v_rows, tables)
    plus_sum, minus_sum, moment_sum, proj_sum = lax.psum(
        (plus_raw, minus_raw, moment_raw, proj_raw), ("bx", "by")
    )
    return (
        v_rows,
        chol_low,
        (plus_sum / row_total, minus_sum / row_total, moment_sum / row_total, proj_sum / row_total),
    )


def transport(factor_k, low_faces, up_faces, ops_list):
    plus_ops, minus_ops, moment_ops, eq_proj = ops_list
    density = jnp.einsum("kj,jxyz->kxyz", moment_ops, factor_k, precision=HIGHEST)
    k_rate = RELAX_RATE * (
        jnp.einsum("mj,mxyz->jxyz", eq_proj, quadratic(density), precision=HIGHEST) - factor_k
    )
    for dim_index in range(3):
        below_k = from_below(factor_k, low_faces[dim_index], dim_index)
        above_k = from_above(factor_k, up_faces[dim_index], dim_index)
        k_rate = (
            k_rate
            - apply_left(plus_ops[dim_index], factor_k - below_k)
            - apply_left(minus_ops[dim_index], above_k - factor_k)
        )
    return factor_k + TIME_STEP * k_rate


def space_basis(new_k, moment_ops, cell_count):
    gram_mat = lax.psum(contract(new_k, new_k), ("bx", "by", "bz"))
    chol_low = jnp.linalg.cholesky(gram_mat / cell_count)
    x_basis = solve_rows(chol_low, new_k)
    low_planes = lower_faces(x_basis)
    coeffs = matmul_hi(moment_ops, chol_low)
    features = quadratic(jnp.einsum("ki,ixyz->kxyz", coeffs, x_basis, precision=HIGHEST))
    shifted_local = jnp.stack(
        [
            contract(x_basis, from_below(x_basis, low_planes[dim_index], dim_index))
            for dim_index in range(3)
        ]
    )
    shifted, moments = lax.psum((shifted_local, contract(features, x_basis)), ("bx", "by", "bz"))
    return (x_basis, chol_low.T, shifted / cell_count, moments / cell_count, low_planes)


def local(space_factor, core_matrix, velocity_factor):
    row_count = velocity_factor.shape[1]
    tables = velocity_tables(lax.axis_index(("bx", "by")) * row_count, row_count)
    speeds = tables[0]
    plus_speed = jnp.maximum(speeds, 0.0)
    minus_speed = jnp.minimum(speeds, 0.0)
    ident_mat = jnp.eye(core_matrix.shape[0], dtype=jnp.float32)
    cell_count = (
        space_factor.shape[1]
        * lax.axis_size("bx")
        * (space_factor.shape[2] * lax.axis_size("by"))
        * (space_factor.shape[3] * lax.axis_size("bz"))
    )
    v_rows, chol_low, ops_list = orthonormal_velocity(velocity_factor, tables, True)
    core_mat = matmul_hi(core_matrix, chol_low)
    x_basis = space_factor
    for turn_index in range(STEPS):
        plus_ops, minus_ops, moment_ops, eq_proj = ops_list
        factor_k = apply_left(core_mat, x_basis)
        low_faces, up_faces = full_rims(factor_k)
        new_k = transport(factor_k, low_faces, up_faces, ops_list)
        x_basis, core_mat, shifted, moments, kept_low = space_basis(new_k, moment_ops, cell_count)
        s_rate = RELAX_RATE * (matmul_hi(moments.T, eq_proj) - core_mat)
        for dim_index in range(3):
            s_rate = s_rate - matmul_hi(
                matmul_hi(ident_mat - shifted[dim_index], core_mat), plus_ops[dim_index]
            )
            s_rate = s_rate - matmul_hi(
                matmul_hi(shifted[dim_index].T - ident_mat, core_mat), minus_ops[dim_index]
            )
        core_mat = core_mat - TIME_STEP * s_rate
        l_factor = matmul_hi(core_mat, v_rows)
        coeffs = matmul_hi(moment_ops, core_mat.T)
        features = quadratic(jnp.einsum("ki,ixyz->kxyz", coeffs, x_basis, precision=HIGHEST))
        collide = lax.psum(contract(features, x_basis), ("bx", "by", "bz")) / cell_count
        l_rate = RELAX_RATE * (matmul_hi(collide.T, tables[1]) - l_factor)
        for dim_index in range(3):
            l_rate = (
                l_rate - matmul_hi(ident_mat - shifted[dim_index], l_factor) * plus_speed[dim_index]
            )
            l_rate = (
                l_rate
                - matmul_hi(shifted[dim_index].T - ident_mat, l_factor) * minus_speed[dim_index]
            )
        l_factor = l_factor + TIME_STEP * l_rate
        v_rows, chol_low, ops_list = orthonormal_velocity(l_factor, tables, turn_index + 1 < STEPS)
        core_mat = chol_low
    return (x_basis, core_mat, v_rows)


def solution(mesh):
    return jax.shard_map(
        local,
        mesh=mesh,
        in_specs=(P(None, "bx", "by", "bz"), P(), P(None, ("bx", "by"))),
        out_specs=(P(None, "bx", "by", "bz"), P(), P(None, ("bx", "by"))),
        check_vma=False,
    )
```

profile of v0, /device:TPU:1, one launch (start us, length us, event | category | flops | bytes accessed | tf_op | source)
XLA Modules:
  0.0 1279.1 jit_solution(10333849148752028989)
XLA Ops:
  8.7 121.8 %psum.133 = f32[64,64]{0,1:T(8,128)S(1)} all-reduce(f32[64,64]{0,1:T(8,128)S(1)} %fusion.327), channel_id=1, replica_groups=mesh['bx'=4,'by'=8,'bz'=8] {'bx','by'}, use_global_device_ids=true, to_apply=%region_0.1 | all-reduce | flops 4096 | bytes 32768 | tf_op jit(solution)/shard_map/psum | solution.py:137
  130.6 5.8 cholesky.89
  137.1 1.6 convolution_bitcast_fusion.10
  139.5 8.2 collective-permute-start.1
  151.1 4.9 custom-call.11
  164.6 108.9 %all-reduce.10.cloned.1.call-done = (f32[4,64]{1,0:T(4,128)}, f32[3,64,64]{2,1,0:T(8,128)}, f32[3,64,64]{2,1,0:T(8,128)}, f32[10,64]{1,0:T(8,128)}) async-done(((f32[4,64]{1,0:T(4,128)}, f32[3,64,64]{2,1,0:T(8,128)}, f32[3,64,64]{2,1,0:T(8,128)}, f32[10,64]{1,0:T(8,128)}), (f32[4,64]{1,0:T(4,128)}, f32[3,64,64]{2,1,0:T(8,128)}, f32[3,64,64]{2,1,0:T(8,128)}, ...) | async-done | bytes 101904 | tf_op jit(solution)/shard_map/psum | solution.py:148
  275.4 1.6 broadcast_multiply_fusion.5
  277.2 2.1 convolution_subtract_fusion.1
  280.3 2.7 collective-permute-start.3
  284.4 1.8 collective-permute-done.2
  289.1 2.4 copy.149
  294.0 1.8 collective-permute-start.5
  296.7 1.7 fusion.45
  302.1 2.0 convolution_subtract_fusion.7
  305.8 76.3 %psum.138 = f32[64,64]{0,1:T(8,128)S(1)} all-reduce(f32[64,64]{0,1:T(8,128)S(1)} %convolution_bitcast_fusion.9), channel_id=1, replica_groups=mesh['bx'=4,'by'=8,'bz'=8] {'bx','by','bz'}, use_global_device_ids=true, to_apply=%region_9.12 | all-reduce | flops 4096 | bytes 32768 | tf_op jit(solution)/shard_map/psum | solution.py:176
  382.2 5.8 cholesky.100
  389.4 4.9 custom-call.12
  397.3 1.7 collective-permute-start.6
  399.8 2.0 collective-permute-start.8
  403.5 11.5 collective-permute-done.8
  416.4 1.6 convolution_bitcast_fusion.8
  418.0 75.6 %all-reduce.2 = (f32[10,64]{1,0:T(8,128)S(1)}, f32[3,64,64]{2,1,0:T(8,128)S(1)}) all-reduce(f32[10,64]{1,0:T(8,128)S(1)} %convolution_bitcast_fusion.14, f32[3,64,64]{2,1,0:T(8,128)S(1)} %pad_maximum_fusion.8), channel_id=1, replica_groups=mesh['bx'=4,'by'=8,'bz'=8] {'bx','by','bz'}, use_global_device_ids=true, to_apply=%region_10.14 | all-reduce | flops 12928 | bytes 103424 | tf_op jit(solution)/shard_map/psum | solution.py:188
  503.8 73.8 %psum.141 = f32[10,64]{1,0:T(8,128)S(1)} all-reduce(f32[10,64]{1,0:T(8,128)S(1)} %convolution_bitcast_fusion.13), channel_id=1, replica_groups=mesh['bx'=4,'by'=8,'bz'=8] {'bx','by','bz'}, use_global_device_ids=true, to_apply=%region_12.16 | all-reduce | flops 640 | bytes 5120 | tf_op jit(solution)/shard_map/psum | solution.py:226
  581.0 117.8 %psum.142 = f32[64,64]{0,1:T(8,128)S(1)} all-reduce(f32[64,64]{0,1:T(8,128)S(1)} %fusion.330), channel_id=1, replica_groups=mesh['bx'=4,'by'=8,'bz'=8] {'bx','by'}, use_global_device_ids=true, to_apply=%region_13.17 | all-reduce | flops 4096 | bytes 32768 | tf_op jit(solution)/shard_map/psum | solution.py:137
  699.0 5.8 cholesky.111
  707.5 4.9 custom-call.13
  719.8 7.9 collective-permute-start.10
  727.7 105.6 %all-reduce.8.cloned.1.call-done = (f32[3,64,64]{2,1,0:T(8,128)}, f32[3,64,64]{2,1,0:T(8,128)}, f32[4,64]{1,0:T(4,128)}, f32[10,64]{1,0:T(8,128)}) async-done(((f32[3,64,64]{2,1,0:T(8,128)}, f32[3,64,64]{2,1,0:T(8,128)}, f32[4,64]{1,0:T(4,128)}, f32[10,64]{1,0:T(8,128)}), (f32[3,64,64]{2,1,0:T(8,128)}, f32[3,64,64]{2,1,0:T(8,128)}, f32[4,64]{1,0:T(4,128)}, f32[10,64]{1,0:T(8,128)})) %all-reduce.8.cloned.1.call-update) | async-done | bytes 101904 | tf_op jit(solution)/shard_map/psum | solution.py:148
  835.2 1.6 broadcast_multiply_fusion.3
  836.9 2.1 convolution_subtract_fusion
  840.1 2.7 collective-permute-start.12
  844.2 1.8 collective-permute-done.11
  848.2 1.8 copy.189
  851.8 2.1 collective-permute-start.14
  854.7 1.7 fusion.68
  860.8 1.9 convolution_subtract_fusion.3
  864.4 76.9 %psum.147 = f32[64,64]{0,1:T(8,128)S(1)} all-reduce(f32[64,64]{0,1:T(8,128)S(1)} %convolution_bitcast_fusion.5), channel_id=1, replica_groups=mesh['bx'=4,'by'=8,'bz'=8] {'bx','by','bz'}, use_global_device_ids=true, to_apply=%region_18.22 | all-reduce | flops 4096 | bytes 32768 | tf_op jit(solution)/shard_map/psum | solution.py:176
  941.4 5.8 cholesky.122
  948.6 4.9 custom-call.14
  956.6 1.7 collective-permute-start.15
  959.0 1.8 collective-permute-start.17
  962.5 11.4 collective-permute-done.17
  975.4 1.6 convolution_bitcast_fusion.4
  977.0 75.7 %all-reduce.1 = (f32[10,64]{1,0:T(8,128)S(1)}, f32[3,64,64]{2,1,0:T(8,128)S(1)}) all-reduce(f32[10,64]{1,0:T(8,128)S(1)} %convolution_bitcast_fusion.12, f32[3,64,64]{2,1,0:T(8,128)S(1)} %pad_maximum_fusion.9), channel_id=1, replica_groups=mesh['bx'=4,'by'=8,'bz'=8] {'bx','by','bz'}, use_global_device_ids=true, to_apply=%region_19.23 | all-reduce | flops 12928 | bytes 103424 | tf_op jit(solution)/shard_map/psum | solution.py:188
  1062.7 73.9 %psum.150 = f32[10,64]{1,0:T(8,128)S(1)} all-reduce(f32[10,64]{1,0:T(8,128)S(1)} %convolution_bitcast_fusion.11), channel_id=1, replica_groups=mesh['bx'=4,'by'=8,'bz'=8] {'bx','by','bz'}, use_global_device_ids=true, to_apply=%region_21.25 | all-reduce | flops 640 | bytes 5120 | tf_op jit(solution)/shard_map/psum | solution.py:226
  1139.9 117.9 %psum.151 = f32[64,64]{0,1:T(8,128)S(1)} all-reduce(f32[64,64]{0,1:T(8,128)S(1)} %fusion.333), channel_id=1, replica_groups=mesh['bx'=4,'by'=8,'bz'=8] {'bx','by'}, use_global_device_ids=true, to_apply=%region_22.26 | all-reduce | flops 4096 | bytes 32768 | tf_op jit(solution)/shard_map/psum | solution.py:137
  1257.9 5.8 cholesky.133
  1265.7 4.9 custom-call.15
  (308 shorter events, 100.7 us)
Async XLA Ops:
  7.2 131.6 %copy-start = (f32[64,2,8,128]{3,2,1,0:T(8,128)S(1)}, f32[64,2,8,128]{3,2,1,0:T(8,128)}, u32[]{:S(2)}) copy-start(f32[64,2,8,128]{3,2,1,0:T(8,128)} %param.8) | copy-start | bytes 1572868
  7.2 266.3 %all-reduce.10.cloned.1.call-start = ((), (), s32[]{:S(2)}) async-start(), calls=%async_computation.1 | async-start | bytes 413696 | tf_op jit(solution)/shard_map/psum | solution.py:148
  130.5 25.5 %copy-start.2 = (f32[64,1024]{1,0:T(8,128)S(1)}, f32[64,1024]{1,0:T(8,128)}, u32[]{:S(2)}) copy-start(f32[64,1024]{1,0:T(8,128)} %param.10) | copy-start | bytes 786436
  139.5 21.7 %copy-start.11 = (f32[64,1,8,128]{3,0,2,1:T(8,128)}, f32[64,1,8,128]{3,0,2,1:T(8,128)S(1)}, u32[]{:S(2)}) copy-start(f32[64,1,8,128]{3,0,2,1:T(8,128)S(1)} %get-tuple-element.47) | copy-start | bytes 786436
  139.5 139.7 %collective-permute-start.1 = (f32[64,1,8,128]{3,0,2,1:T(8,128)S(1)}, f32[64,1,8,128]{3,0,2,1:T(8,128)S(1)}, u32[]{:S(2)}, u32[]{:S(2)}) collective-permute-start(f32[64,1,8,128]{3,0,2,1:T(8,128)S(1)} %get-tuple-element.47), channel_id=1, source_target_pairs={{64,0},{128,64},{192,128},{0,192},{65,1},{129,65},{193,129},{1,193... | collective-permute-start | bytes 786440 | tf_op jit(solution)/shard_map/ppermute | solution.py:30
  147.7 131.6 %collective-permute-start = (f32[64,1,8,128]{3,0,2,1:T(8,128)S(1)}, f32[64,1,8,128]{3,0,2,1:T(8,128)S(1)}, u32[]{:S(2)}, u32[]{:S(2)}) collective-permute-start(f32[64,1,8,128]{3,0,2,1:T(8,128)S(1)} %get-tuple-element.46), channel_id=1, source_target_pairs={{0,64},{64,128},{128,192},{192,0},{1,65},{65,129},{129,193},{193,1... | collective-permute-start | bytes 786440 | tf_op jit(solution)/shard_map/ppermute | solution.py:29
  161.2 672.0 %all-reduce.8.cloned.1.call-start = ((), (), s32[]{:S(2)}) async-start(), calls=%async_computation | async-start | bytes 413696 | tf_op jit(solution)/shard_map/psum | solution.py:148
  275.4 7.5 copy-start.15
  279.3 6.9 collective-permute-start.2
  280.3 5.9 collective-permute-start.3
  291.5 9.4 collective-permute-start.4
  294.0 4.4 copy-start.3
  294.0 4.4 copy-start.5
  294.0 4.4 copy-start.12
  294.0 4.4 copy-start.19
  294.0 7.8 collective-permute-start.5
  397.3 19.1 %collective-permute-start.6 = (f32[64,1,8,128]{3,0,2,1:T(8,128)}, f32[64,1,8,128]{3,0,2,1:T(8,128)}, u32[]{:S(2)}, u32[]{:S(2)}) collective-permute-start(f32[64,1,8,128]{3,0,2,1:T(8,128)} %copy.338), channel_id=1, source_target_pairs={{192,0},{0,64},{64,128},{128,192},{193,1},{1,65},{65,129},{129,193... | collective-permute-start | bytes 786440 | tf_op jit(solution)/shard_map/ppermute | solution.py:19
  399.7 16.0 %collective-permute-start.7 = (f32[64,2,1,128]{3,0,2,1:T(8,128)}, f32[64,2,1,128]{3,0,2,1:T(8,128)S(1)}, u32[]{:S(2)}, u32[]{:S(2)}) collective-permute-start(f32[64,2,1,128]{3,0,2,1:T(8,128)} %copy.336), channel_id=1, source_target_pairs={{56,0},{0,8},{8,16},{16,24},{24,32},{32,40},{40,48},{48,56},{57,1}... | collective-permute-start | bytes 196616 | tf_op jit(solution)/shard_map/ppermute | solution.py:19
  399.8 15.1 %collective-permute-start.8 = (f32[64,2,8,1]{3,0,2,1:T(8,128)S(1)}, f32[64,2,8,1]{3,0,2,1:T(8,128)S(1)}, u32[]{:S(2)}, u32[]{:S(2)}) collective-permute-start(f32[64,2,8,1]{3,0,2,1:T(8,128)S(1)} %copy.334), channel_id=1, source_target_pairs={{7,0},{0,1},{1,2},{2,3},{3,4},{4,5},{5,6},{6,7},{15,8},{8,9},{9,10... | collective-permute-start | bytes 12296 | tf_op jit(solution)/shard_map/ppermute | solution.py:19
  416.4 82.6 %copy-start.37 = (f32[10,64]{1,0:T(8,128)S(1)}, f32[10,64]{1,0:T(8,128)}, u32[]{:S(2)}) copy-start(f32[10,64]{1,0:T(8,128)} %get-tuple-element.17) | copy-start | bytes 7684
  502.2 75.9 %copy-start.33 = (f32[1,1024]{1,0:T(1,128)S(1)}, f32[1,1024]{1,0:T(1,128)}, u32[]{:S(2)}) copy-start(f32[1,1024]{1,0:T(1,128)} %get-tuple-element.97) | copy-start | bytes 12292
  503.1 75.4 %copy-start.35 = (f32[1,1024]{1,0:T(1,128)S(1)}, f32[1,1024]{1,0:T(1,128)}, u32[]{:S(2)}) copy-start(f32[1,1024]{1,0:T(1,128)} %get-tuple-element.94) | copy-start | bytes 12292
  503.8 75.1 %copy-start.29 = (f32[1,1024]{1,0:T(1,128)S(1)}, f32[1,1024]{1,0:T(1,128)}, u32[]{:S(2)}) copy-start(f32[1,1024]{1,0:T(1,128)} %get-tuple-element.96) | copy-start | bytes 12292
  578.5 1.3 copy-start.25
  578.9 1.3 copy-start.27
  719.8 119.3 %copy-start.13 = (f32[64,1,8,128]{3,0,2,1:T(8,128)}, f32[64,1,8,128]{3,0,2,1:T(8,128)S(1)}, u32[]{:S(2)}) copy-start(f32[64,1,8,128]{3,0,2,1:T(8,128)S(1)} %get-tuple-element.39) | copy-start | bytes 786436
  719.8 119.3 %collective-permute-start.10 = (f32[64,1,8,128]{3,0,2,1:T(8,128)S(1)}, f32[64,1,8,128]{3,0,2,1:T(8,128)S(1)}, u32[]{:S(2)}, u32[]{:S(2)}) collective-permute-start(f32[64,1,8,128]{3,0,2,1:T(8,128)S(1)} %get-tuple-element.39), channel_id=1, source_target_pairs={{64,0},{128,64},{192,128},{0,192},{65,1},{129,65},{193,129},{1,193... | collective-permute-start | bytes 786440 | tf_op jit(solution)/shard_map/ppermute | solution.py:30
  727.7 111.4 %collective-permute-start.9 = (f32[64,1,8,128]{3,0,2,1:T(8,128)S(1)}, f32[64,1,8,128]{3,0,2,1:T(8,128)S(1)}, u32[]{:S(2)}, u32[]{:S(2)}) collective-permute-start(f32[64,1,8,128]{3,0,2,1:T(8,128)S(1)} %get-tuple-element.38), channel_id=1, source_target_pairs={{0,64},{64,128},{128,192},{192,0},{1,65},{65,129},{129,193},{193,1... | collective-permute-start | bytes 786440 | tf_op jit(solution)/shard_map/ppermute | solution.py:29
  835.2 7.6 copy-start.17
  839.1 6.9 collective-permute-start.11
  840.1 5.9 collective-permute-start.12
  850.0 8.9 collective-permute-start.13
  851.7 4.6 copy-start.4
  851.8 4.6 copy-start.6
  851.8 4.6 copy-start.14
  851.8 4.6 copy-start.20
  851.8 8.0 collective-permute-start.14
  857.4 3.4 copy-start.8
  860.8 1.9 copy-start.7
  954.3 107.8 %copy-start.1 = (f32[8,8,16,128]{3,2,1,0:T(8,128)}, f32[8,8,16,128]{3,2,1,0:T(8,128)S(1)}, u32[]{:S(2)}) copy-start(f32[8,8,16,128]{3,2,1,0:T(8,128)S(1)} %copy.292) | copy-start | bytes 1572868
  956.6 18.8 %collective-permute-start.15 = (f32[64,1,8,128]{3,0,2,1:T(8,128)}, f32[64,1,8,128]{3,0,2,1:T(8,128)}, u32[]{:S(2)}, u32[]{:S(2)}) collective-permute-start(f32[64,1,8,128]{3,0,2,1:T(8,128)} %copy.344), channel_id=1, source_target_pairs={{192,0},{0,64},{64,128},{128,192},{193,1},{1,65},{65,129},{129,193... | collective-permute-start | bytes 786440 | tf_op jit(solution)/shard_map/ppermute | solution.py:19
  958.9 15.8 %collective-permute-start.16 = (f32[64,2,1,128]{3,0,2,1:T(8,128)}, f32[64,2,1,128]{3,0,2,1:T(8,128)S(1)}, u32[]{:S(2)}, u32[]{:S(2)}) collective-permute-start(f32[64,2,1,128]{3,0,2,1:T(8,128)} %copy.342), channel_id=1, source_target_pairs={{56,0},{0,8},{8,16},{16,24},{24,32},{32,40},{40,48},{48,56},{57,1}... | collective-permute-start | bytes 196616 | tf_op jit(solution)/shard_map/ppermute | solution.py:19
  959.0 14.9 %collective-permute-start.17 = (f32[64,2,8,1]{3,0,2,1:T(8,128)S(1)}, f32[64,2,8,1]{3,0,2,1:T(8,128)S(1)}, u32[]{:S(2)}, u32[]{:S(2)}) collective-permute-start(f32[64,2,8,1]{3,0,2,1:T(8,128)S(1)} %copy.340), channel_id=1, source_target_pairs={{7,0},{0,1},{1,2},{2,3},{3,4},{4,5},{5,6},{6,7},{15,8},{8,9},{9,10... | collective-permute-start | bytes 12296 | tf_op jit(solution)/shard_map/ppermute | solution.py:19
  975.4 82.5 %copy-start.38 = (f32[10,64]{1,0:T(8,128)S(1)}, f32[10,64]{1,0:T(8,128)}, u32[]{:S(2)}) copy-start(f32[10,64]{1,0:T(8,128)} %get-tuple-element.13) | copy-start | bytes 7684
  1061.1 76.0 %copy-start.34 = (f32[1,1024]{1,0:T(1,128)S(1)}, f32[1,1024]{1,0:T(1,128)}, u32[]{:S(2)}) copy-start(f32[1,1024]{1,0:T(1,128)} %get-tuple-element.97) | copy-start | bytes 12292
  1062.0 75.4 %copy-start.36 = (f32[1,1024]{1,0:T(1,128)S(1)}, f32[1,1024]{1,0:T(1,128)}, u32[]{:S(2)}) copy-start(f32[1,1024]{1,0:T(1,128)} %get-tuple-element.94) | copy-start | bytes 12292
  1062.7 75.1 %copy-start.30 = (f32[1,1024]{1,0:T(1,128)S(1)}, f32[1,1024]{1,0:T(1,128)}, u32[]{:S(2)}) copy-start(f32[1,1024]{1,0:T(1,128)} %get-tuple-element.96) | copy-start | bytes 12292
  1137.4 1.3 copy-start.26
  (15 other events, 13.7 us)
Sparse Core Ops, SparseCore 0:
  161.3 112.0 all-reduce.9
  719.8 113.3 all-reduce.7
where the time goes:
time: 1290 us; the launch traced here: 1280 us
  blocking collectives  810 us (63%)
  waiting for transfers between devices  241 us (19%)
  matrix products  76.8 us (6%)
  other arithmetic  67.2 us (5%)
  starting transfers between devices  37.3 us (3%)
  local copies, waits for them, and re-layouts  29 us (2%)
  between operations  18 us (1%)
    psum x3, blocking collectives, plain_velocity(): gram_mat = lax.psum(matmul_hi(raw_rows, raw_rows.T), ('bx', 'by'))  358 us
    psum x2, waiting for transfers between devices, orthonormal_velocity(): lax.psum((plus_raw, minus_raw, moment_raw, proj_raw), ('bx', 'by'))  214 us
    psum x2, blocking collectives, space_basis(): gram_mat = lax.psum(contract(new_k, new_k), ('bx', 'by', 'bz'))  153 us
    psum x2, blocking collectives, space_basis(): lax.psum((shifted_local, contract(features, x_basis)), ('bx', 'by', 'bz'))  151 us
    psum x2, blocking collectives, local(): lax.psum(contract(features, x_basis), ('bx', 'by', 'bz')) / cell_count  148 us
    dot_general x54, matrix products, matmul_hi(): return jnp.dot(left_mat, right_mat, precision=HIGHEST)  32 us
  transfers between devices with their start and end apart: 20, of which 6 were waited for; matrix products, arithmetic and copies ran while one was open for 4% of the time, Pallas kernels for 0%

commit v1 on v0

v1 whole, which is shorter than its diff:
```python
import jax
import jax.numpy as jnp
import numpy as np
from jax import lax
from jax.sharding import PartitionSpec as P

VEL_N = 32
STEPS = 2
TIME_STEP = 0.1
SPEED_MAX = 3.0
HIGHEST = lax.Precision.HIGHEST
PLANE = ("bx", "by")


def mm(a, b):
    return jnp.dot(a, b, precision=HIGHEST)


def mmt(a, b):
    return lax.dot_general(a, b, (((1,), (1,)), ((), ())), precision=HIGHEST)


def velocity_tables(start, row_count, xp=jnp):
    row_ids = start + xp.arange(row_count, dtype=xp.int32)
    levels = xp.stack(
        [row_ids // (VEL_N * VEL_N), row_ids // VEL_N % VEL_N, row_ids % VEL_N]
    ).astype(xp.float32)
    speeds = SPEED_MAX * (2.0 * levels + 1.0 - VEL_N) / VEL_N
    line = SPEED_MAX * (2.0 * xp.arange(VEL_N, dtype=xp.float32) + 1.0 - VEL_N) / VEL_N
    norm_one = xp.mean(xp.exp(-0.5 * line * line))
    weight = xp.exp(-0.5 * xp.sum(speeds * speeds, axis=0)) / (norm_one * norm_one * norm_one)
    modes = xp.stack(
        [
            weight,
            weight * speeds[0],
            weight * speeds[1],
            weight * speeds[2],
            0.5 * weight * (speeds[0] * speeds[0] - 1.0),
            0.5 * weight * (speeds[1] * speeds[1] - 1.0),
            0.5 * weight * (speeds[2] * speeds[2] - 1.0),
            weight * speeds[0] * speeds[1],
            weight * speeds[0] * speeds[2],
            weight * speeds[1] * speeds[2],
        ]
    )
    moment_rows = xp.concatenate([xp.ones_like(speeds[:1]), speeds], axis=0)
    return (speeds, modes, moment_rows)


def face_weights(speeds, xp=jnp):
    rows = [xp.ones_like(speeds[0])]
    for d in range(3):
        rows += [xp.maximum(speeds[d], 0.0), xp.minimum(speeds[d], 0.0)]
    return xp.stack(rows)


def grid_constants(row_total):
    speeds, modes, moments = velocity_tables(0, row_total, np)
    modes = modes.astype(np.float64)
    weights = face_weights(speeds, np).astype(np.float64)
    mode_gram = np.einsum("wv,mv,nv->wmn", weights, modes, modes)
    return mode_gram.astype(np.float32), (moments.astype(np.float64) @ modes.T).astype(np.float32)


def quadratic(d):
    return jnp.concatenate(
        [d, d[1:4] * d[1:4], d[1:2] * d[2:3], d[1:2] * d[3:4], d[2:3] * d[3:4]], axis=0
    )


def route(axis, step):
    n = lax.axis_size(axis)
    return [(i, (i + step) % n) for i in range(n)]


def swap(chunks, axis):
    return lax.all_to_all(chunks, axis, 0, 0, tiled=True)


def total(payload, over_z):
    n = lax.axis_size(PLANE)
    rows = payload.shape[0] // n
    part = jnp.sum(swap(payload.reshape(n, rows, 128), PLANE), axis=0)
    if over_z:
        nz = lax.axis_size("bz")
        part = jnp.sum(swap(jnp.broadcast_to(part[None], (nz, rows, 128)), "bz"), axis=0)
    return swap(jnp.broadcast_to(part[None], (n, rows, 128)), PLANE).reshape(n * rows, 128)


def pack(mats, rows):
    flat = jnp.concatenate(mats, axis=0)
    pad = 2 * rows - flat.shape[0]
    flat = jnp.concatenate([flat, jnp.zeros((pad, 64), jnp.float32)], axis=0)
    return jnp.concatenate([flat[:rows], flat[rows:]], axis=1)


def unpack(payload, counts):
    flat = jnp.concatenate([payload[:, :64], payload[:, 64:]], axis=0)
    out, at = [], 0
    for c in counts:
        out.append(flat[at : at + c])
        at += c
    return out


def planes(field):
    low = (
        lax.ppermute(field[:, -1:], "bx", route("bx", 1)),
        lax.ppermute(field[:, :, -1:], "by", route("by", 1)),
        lax.ppermute(field[:, :, :, -1:], "bz", route("bz", 1)),
    )
    high = (
        lax.ppermute(field[:, :1], "bx", route("bx", -1)),
        lax.ppermute(field[:, :, :1], "by", route("by", -1)),
        lax.ppermute(field[:, :, :, :1], "bz", route("bz", -1)),
    )
    return low, high


def below(field, plane, d):
    n = field.shape[d + 1]
    return jnp.concatenate([plane, lax.slice_in_dim(field, 0, n - 1, axis=d + 1)], axis=d + 1)


def above(field, plane, d):
    n = field.shape[d + 1]
    return jnp.concatenate([lax.slice_in_dim(field, 1, n, axis=d + 1), plane], axis=d + 1)


def flat(field):
    return field.reshape(field.shape[0], -1)


def chol_inverse(gram):
    low = jnp.linalg.cholesky(gram)
    inv = jax.scipy.linalg.solve_triangular(low, jnp.eye(gram.shape[0], dtype=gram.dtype), lower=True)
    return low, inv


def weighted(rows_l, modes, weights, moments):
    stack = (rows_l[None] * weights[:, None, :]).reshape(-1, rows_l.shape[1])
    quads = mmt(stack, rows_l)
    mode_stack = (modes[None] * weights[:, None, :]).reshape(-1, rows_l.shape[1])
    return quads, mmt(mode_stack, rows_l), mmt(moments, rows_l)


def operators(grams, modes_raw, moments_raw, count):
    low, inv = chol_inverse(grams[0] / count)
    side = mm(inv, grams[1:].transpose(1, 0, 2).reshape(64, -1)).reshape(64, 6, 64)
    ops = mmt(side.reshape(-1, 64), inv).reshape(64, 6, 64).transpose(1, 0, 2) / count
    return low, inv, ops, mmt(moments_raw, inv) / count, mmt(modes_raw, inv) / count


def local(space_factor, core_matrix, velocity_factor):
    rows = velocity_factor.shape[1]
    n_plane = lax.axis_size(PLANE)
    vel_count = rows * n_plane
    nz = lax.axis_size("bz")
    speeds, modes, moments = velocity_tables(lax.axis_index(PLANE) * rows, rows)
    weights = face_weights(speeds)
    mode_gram, moment_mode = grid_constants(vel_count)
    ident = jnp.eye(64, dtype=jnp.float32)
    shape = space_factor.shape
    cells = shape[1] * shape[2] * shape[3] * lax.axis_size("bx") * lax.axis_size("by") * nz

    field = space_factor
    low, high = planes(field)
    quads, mode_rows, moment_sums = weighted(velocity_factor, modes, weights, moments)
    sums = total(pack([quads, mode_rows[:10], moment_sums], 256), False)
    quads, mode_rows, moment_sums = unpack(sums, (448, 10, 4))
    c_vel, c_vel_inv, ops, mu, proj = operators(
        quads.reshape(7, 64, 64), mode_rows, moment_sums, vel_count
    )
    rows_l = velocity_factor
    turn_map = mm(core_matrix, c_vel).T
    for turn in range(STEPS):
        rows_v = mm(c_vel_inv, rows_l)
        plus, minus = ops[0::2], ops[1::2]
        stay = (1.0 - TIME_STEP) * ident + TIME_STEP * jnp.sum(minus - plus, axis=0)
        maps = [mm(stay, turn_map)]
        maps += [mm(TIME_STEP * plus[d], turn_map) for d in range(3)]
        maps += [mm(-TIME_STEP * minus[d], turn_map) for d in range(3)]
        feats = quadratic(mm(mm(mu, turn_map), flat(field)))
        parts = [flat(field)]
        parts += [flat(below(field, low[d], d)) for d in range(3)]
        parts += [flat(above(field, high[d], d)) for d in range(3)]
        new_k = mm(
            jnp.concatenate(maps + [TIME_STEP * proj.T], axis=1),
            jnp.concatenate(parts + [feats], axis=0),
        )
        field = new_k.reshape(shape)
        low, high = planes(field)
        feats = quadratic(mm(mu, new_k))
        right = [new_k] + [flat(below(field, low[d], d)) for d in range(3)] + [feats]
        sums = total(pack([mmt(jnp.concatenate(right, axis=0), new_k)], 256), True) / cells
        gram, shifts, moment_x = unpack(sums, (64, 192, 10))
        c_x, c_x_inv = chol_inverse(gram)
        sh_t = [mmt(mm(c_x_inv, shifts[64 * d : 64 * d + 64]), c_x_inv) for d in range(3)]
        moment_x = mmt(moment_x, c_x_inv)
        core = c_x.T
        rate = mm(moment_x.T, proj) - core
        for d in range(3):
            rate = rate - mm(mm(ident - sh_t[d].T, core), plus[d])
            rate = rate - mm(mm(sh_t[d] - ident, core), minus[d])
        core = core - TIME_STEP * rate
        coeffs = mmt(mu, core)
        feats = quadratic(mm(mm(coeffs, c_x_inv), new_k))
        collide = mmt(feats, new_k)
        sv = mm(core, rows_v)
        steps = [(1.0 - TIME_STEP) * ident]
        for d in range(3):
            steps += [-TIME_STEP * (ident - sh_t[d].T), -TIME_STEP * (sh_t[d] - ident)]
        sv_stack = (sv[None] * weights[:, None, :]).reshape(-1, rows)
        rows_a = mm(jnp.concatenate(steps, axis=1), sv_stack)
        last = turn + 1 == STEPS
        if last:
            quads, mode_rows = mmt(rows_a, rows_a), mmt(modes, rows_a)
            mats = [quads / nz, mode_rows / nz, collide]
            quads, mode_rows, collide = unpack(total(pack(mats, 256), True), (64, 10, 10))
        else:
            quads, mode_rows, moment_sums = weighted(rows_a, modes, weights, moments)
            mats = [quads / nz, mode_rows / nz, moment_sums / nz, collide]
            quads, mode_rows, moment_sums, collide = unpack(
                total(pack(mats, 512), True), (448, 70, 4, 10)
            )
        gain = TIME_STEP * mmt(collide / cells, c_x_inv).T
        rows_l = rows_a + mm(gain, modes)
        if last:
            cross = mm(gain, mode_rows)
            grams = quads + cross + cross.T + mm(gain, mmt(mode_gram[0], gain))
            c_vel, c_vel_inv = chol_inverse(grams / vel_count)
            return (mm(c_x_inv, new_k).reshape(shape), c_vel, mm(c_vel_inv, rows_l))
        mode_rows = mode_rows.reshape(7, 10, 64)
        grams = []
        for w in range(7):
            cross = mm(gain, mode_rows[w])
            grams.append(quads[64 * w : 64 * w + 64] + cross + cross.T + mm(gain, mmt(mode_gram[w], gain)))
        c_vel, c_vel_inv, ops, mu, proj = operators(
            jnp.stack(grams),
            mode_rows[0] + mmt(mode_gram[0], gain),
            moment_sums + mmt(moment_mode, gain),
            vel_count,
        )
        turn_map = mm(c_vel.T, c_x_inv)


def solution(mesh):
    return jax.shard_map(
        local,
        mesh=mesh,
        in_specs=(P(None, "bx", "by", "bz"), P(), P(None, PLANE)),
        out_specs=(P(None, "bx", "by", "bz"), P(), P(None, PLANE)),
        check_vma=False,
    )
```

time: 1290 us -> 466 us (0.36)
  blocking collectives: 810 us -> 32.9 us
  waiting for transfers between devices: 241 us -> 99.4 us
  starting transfers between devices: 37.3 us -> 86.5 us
  local copies, waits for them, and re-layouts: 29 us -> 73.9 us
  between operations: 18 us -> 4.69 us
  other arithmetic: 67.2 us -> 80.2 us
    psum x9 -> x0, blocking collectives: 810 us -> none  [the longest x3 358 us: plain_velocity(): gram_mat = lax.psum(matmul_hi(raw_rows, raw_rows.T), ('bx', 'by'))]
    psum x2 -> x0, waiting for transfers between devices: 214 us -> none  [orthonormal_velocity(): lax.psum((plus_raw, minus_raw, moment_raw, proj_raw), ('bx', 'by'))]
    all_to_all x0 -> x11, starting transfers between devices: none -> 64.5 us  [swap(): return lax.all_to_all(chunks, axis, 0, 0, tiled=True)]
    all_to_all x0 -> x11, waiting for transfers between devices: none -> 59.9 us  [swap(): return lax.all_to_all(chunks, axis, 0, 0, tiled=True)]
    all_to_all x0 -> x3, blocking collectives: none -> 32.9 us  [swap(): return lax.all_to_all(chunks, axis, 0, 0, tiled=True)]
    concatenate x0 -> x12, local copies, waits for them, and re-layouts: none -> 31.5 us  [the longest x2 19.7 us: local(): jnp.concatenate(parts + [feats], axis=0)]
    ppermute x18 -> x15, starting transfers between devices: 37.3 us -> 21.9 us  [the longest x2 6.83 us: planes(): lax.ppermute(field[:, :, :, :1], 'bz', route('bz', -1))]
    ppermute x18 -> x15, waiting for transfers between devices: 26.5 us -> 39.5 us  [the longest x3 37.7 us: planes(): lax.ppermute(field[:, :, :, -1:], 'bz', route('bz', 1))]
  transfers between devices with their start and end apart: 20 -> 26, of which waited for: 6 -> 14; matrix products, arithmetic and copies ran while one was open for 4% -> 14% of each run, Pallas kernels for 0% -> 0%
where the time goes in v1:
time: 466 us; the launch traced here: 460 us
  waiting for transfers between devices  99.4 us (21%)
  starting transfers between devices  86.5 us (19%)
  matrix products  82.6 us (18%)
  other arithmetic  80.2 us (17%)
  local copies, waits for them, and re-layouts  73.9 us (16%)
  blocking collectives  32.9 us (7%)
  between operations  4.69 us (1%)
    all_to_all x11, starting transfers between devices, swap(): return lax.all_to_all(chunks, axis, 0, 0, tiled=True)  64.5 us
    dot_general x88, matrix products, mm(): return jnp.dot(a, b, precision=HIGHEST)  60 us
    all_to_all x11, waiting for transfers between devices, swap(): return lax.all_to_all(chunks, axis, 0, 0, tiled=True)  59.9 us
    ppermute x3, waiting for transfers between devices, planes(): lax.ppermute(field[:, :, :, -1:], 'bz', route('bz', 1))  37.7 us
    another operation x15, other arithmetic, chol_inverse(): low = jnp.linalg.cholesky(gram)  33.4 us
    all_to_all x3, blocking collectives, swap(): return lax.all_to_all(chunks, axis, 0, 0, tiled=True)  32.9 us
    another operation x10, other arithmetic, chol_inverse(): jax.scipy.linalg.solve_triangular(low, jnp.eye(gram.shape[0], dtype=gram....  30.3 us
    dot_general x39, matrix products, mmt(): return lax.dot_general(a, b, (((1,), (1,)), ((), ())), precision=HIGHEST)  20.6 us
  transfers between devices with their start and end apart: 26, of which 14 were waited for; matrix products, arithmetic and copies ran while one was open for 14% of the time, Pallas kernels for 0%

profile of v1, /device:TPU:1, one launch (start us, length us, event | category | flops | bytes accessed | tf_op | source)
XLA Modules:
  0.0 460.2 jit_solution(11605642236537980220)
XLA Ops:
  9.3 8.6 %all-to-all-start = ((f32[32,8,128]{2,1,0:T(8,128)}), f32[32,8,128]{2,1,0:T(8,128)}, u32[]{:S(2)}, u32[]{:S(2)}) async-start(f32[32,8,128]{2,1,0:T(8,128)} %bitcast.2), calls=%async_computation | async-start | bytes 262144 | tf_op jit(solution)/shard_map/all_to_all | solution.py:77
  19.1 2.9 collective-permute-start
  26.1 4.0 collective-permute-start.5
  30.5 11.6 %collective-permute-done.2 = f32[64,2,8,1]{3,2,1,0:T(8,128)S(1)} collective-permute-done((f32[64,2,8,1]{3,2,1,0:T(8,128)S(1)}, f32[64,2,8,1]{3,2,1,0:T(8,128)S(1)}, u32[]{:S(2)}, u32[]{:S(2)}) %collective-permute-start.2) | collective-permute-done | bytes 4128 | tf_op jit(solution)/shard_map/ppermute | solution.py:110
  46.5 5.8 %all-to-all-start.1 = ((f32[32,8,128]{2,1,0:T(8,128)}), f32[32,8,128]{2,1,0:T(8,128)}, u32[]{:S(2)}, u32[]{:S(2)}) async-start(f32[32,8,128]{2,1,0:T(8,128)} %broadcast_in_dim.26), calls=%async_computation.1 | async-start | bytes 262144 | tf_op jit(solution)/shard_map/all_to_all | solution.py:77
  53.8 6.0 %all-to-all-done.1 = f32[32,8,128]{2,1,0:T(8,128)} async-done(((f32[32,8,128]{2,1,0:T(8,128)}), f32[32,8,128]{2,1,0:T(8,128)}, u32[]{:S(2)}, u32[]{:S(2)}) %all-to-all-start.1) | async-done | bytes 131104 | tf_op jit(solution)/shard_map/all_to_all | solution.py:77
  67.2 6.6 %cholesky.89 = f32[64,64]{1,0:T(8,128)S(1)} custom-call(f32[64,64]{1,0:T(8,128)} %fusion.66), custom_call_target="Cholesky" | custom-call | tf_op jit(solution)/shard_map/jit(cholesky)/cholesky | solution.py:135
  82.6 6.3 %custom-call.9 = f32[1,64,64]{1,2,0:T(8,128)} custom-call(f32[1,64,64]{2,1,0:T(8,128)} %fusion.76), custom_call_target="InvertDiagBlocksLowerTriangular" | custom-call | tf_op jit(solution)/shard_map/jit(_solve_triangular)/triangular_solve | solution.py:136
  108.1 9.8 %concatenate.134 = f32[458,2048]{1,0:T(8,128)} concatenate(f32[64,2048]{1,0:T(8,128)S(1)} %bitcast.562, f32[64,2048]{1,0:T(8,128)} %get-tuple-element.110, f32[64,2048]{1,0:T(8,128)S(1)} %bitcast.565, f32[64,2048]{1,0:T(8,128)S(1)} %bitcast.563, f32[64,2048]{1,0:T(8,128)S(1)} %get-tuple-element.109, f32[64,2048]{1,0:T(8,128)S(1)} %bitcast.566, f32[64,2048]{1,0:T(8,128)S(1)} %bitcast.564, ...), dimensions={0} | concatenate | bytes 7503872 | tf_op jit(solution)/shard_map/concatenate | solution.py:189
  117.9 4.6 fusion.253
  128.7 13.2 %collective-permute-done.8 = f32[64,2,8,1]{3,2,1,0:T(8,128)S(1)} collective-permute-done((f32[64,2,8,1]{3,2,1,0:T(8,128)S(1)}, f32[64,2,8,1]{3,2,1,0:T(8,128)S(1)}, u32[]{:S(2)}, u32[]{:S(2)}) %collective-permute-start.8) | collective-permute-done | bytes 4128 | tf_op jit(solution)/shard_map/ppermute | solution.py:110
  145.2 3.4 concatenate.138
  148.6 2.4 fusion.255
  151.7 3.6 all-to-all-start.2
  155.4 7.6 %all-to-all-done.2 = f32[32,8,128]{2,1,0:T(8,128)S(1)} async-done(((f32[32,8,128]{2,1,0:T(8,128)}), f32[32,8,128]{2,1,0:T(8,128)S(1)}, u32[]{:S(2)}, u32[]{:S(2)}) %all-to-all-start.2) | async-done | bytes 131104 | tf_op jit(solution)/shard_map/all_to_all | solution.py:77
  163.6 5.4 %all-to-all-start.3 = ((f32[8,8,128]{2,1,0:T(8,128)}), f32[8,8,128]{2,1,0:T(8,128)S(1)}, u32[]{:S(2)}, u32[]{:S(2)}) async-start(f32[8,8,128]{2,1,0:T(8,128)} %broadcast_in_dim.27), calls=%async_computation.3 | async-start | bytes 65536 | tf_op jit(solution)/shard_map/all_to_all | solution.py:77
  169.1 6.8 %all-to-all-done.3 = f32[8,8,128]{2,1,0:T(8,128)S(1)} async-done(((f32[8,8,128]{2,1,0:T(8,128)}), f32[8,8,128]{2,1,0:T(8,128)S(1)}, u32[]{:S(2)}, u32[]{:S(2)}) %all-to-all-start.3) | async-done | bytes 32800 | tf_op jit(solution)/shard_map/all_to_all | solution.py:77
  176.6 14.0 %all-to-all-start.4 = ((f32[32,8,128]{2,1,0:T(8,128)}), f32[32,8,128]{2,1,0:T(8,128)S(1)}, u32[]{:S(2)}, u32[]{:S(2)}) async-start(f32[32,8,128]{2,1,0:T(8,128)} %broadcast_in_dim.28), calls=%async_computation.4 | async-start | bytes 262144 | tf_op jit(solution)/shard_map/all_to_all | solution.py:77
  191.0 7.1 %all-to-all-done.4 = f32[32,8,128]{2,1,0:T(8,128)S(1)} async-done(((f32[32,8,128]{2,1,0:T(8,128)}), f32[32,8,128]{2,1,0:T(8,128)S(1)}, u32[]{:S(2)}, u32[]{:S(2)}) %all-to-all-start.4) | async-done | bytes 131104 | tf_op jit(solution)/shard_map/all_to_all | solution.py:77
  198.2 5.8 %cholesky.100 = f32[64,64]{1,0:T(8,128)S(1)} custom-call(f32[64,64]{1,0:T(8,128)S(1)} %fusion.61), custom_call_target="Cholesky" | custom-call | tf_op jit(solution)/shard_map/jit(cholesky)/cholesky | solution.py:135
  205.4 4.9 %custom-call.10 = f32[1,64,64]{1,2,0:T(8,128)S(1)} custom-call(f32[1,64,64]{2,1,0:T(8,128)S(1)} %fusion.75), custom_call_target="InvertDiagBlocksLowerTriangular" | custom-call | tf_op jit(solution)/shard_map/jit(_solve_triangular)/triangular_solve | solution.py:136
  226.8 12.4 %all_to_all.70 = f32[32,16,128]{2,1,0:T(8,128)S(1)} all-to-all(f32[32,16,128]{2,1,0:T(8,128)S(1)} %bitcast.585), channel_id=1, replica_groups=mesh['bx'=4,'by'=8,'bz'=8] {'bx','by'}, dimensions={0} | all-to-all | bytes 524288 | tf_op jit(solution)/shard_map/all_to_all | solution.py:77
  239.9 3.3 all-to-all-start.6
  243.8 2.8 collective-permute-start.11
  247.9 2.5 all-to-all-done.6
  251.1 5.6 %all-to-all-start.7 = ((f32[32,16,128]{2,1,0:T(8,128)}), f32[32,16,128]{2,1,0:T(8,128)S(1)}, u32[]{:S(2)}, u32[]{:S(2)}) async-start(f32[32,16,128]{2,1,0:T(8,128)} %broadcast_in_dim.31), calls=%async_computation.7 | async-start | bytes 524288 | tf_op jit(solution)/shard_map/all_to_all | solution.py:77
  263.0 2.5 all-to-all-done.7
  268.0 5.8 %cholesky.111 = f32[64,64]{1,0:T(8,128)S(1)} custom-call(f32[64,64]{1,0:T(8,128)S(1)} %fusion.59), custom_call_target="Cholesky" | custom-call | tf_op jit(solution)/shard_map/jit(cholesky)/cholesky | solution.py:135
  284.9 4.9 %custom-call.11 = f32[1,64,64]{1,2,0:T(8,128)S(1)} custom-call(f32[1,64,64]{2,1,0:T(8,128)S(1)} %fusion.74), custom_call_target="InvertDiagBlocksLowerTriangular" | custom-call | tf_op jit(solution)/shard_map/jit(_solve_triangular)/triangular_solve | solution.py:136
  306.0 9.9 %concatenate.151 = f32[458,2048]{1,0:T(8,128)} concatenate(f32[64,2048]{1,0:T(8,128)S(1)} %fusion.253, f32[64,2048]{1,0:T(8,128)S(1)} %bitcast.547, f32[64,2048]{1,0:T(8,128)S(1)} %bitcast.545, f32[64,2048]{1,0:T(8,128)S(1)} %bitcast.543, f32[64,2048]{1,0:T(8,128)} %bitcast.561, f32[64,2048]{1,0:T(8,128)} %bitcast.560, f32[64,2048]{1,0:T(8,128)S(1)} %bitcast.559, ...), dimensions={0} | concatenate | bytes 7503872 | tf_op jit(solution)/shard_map/concatenate | solution.py:189
  316.8 4.5 fusion.272
  325.0 12.9 %collective-permute-done.14 = f32[64,2,8,1]{3,2,1,0:T(8,128)S(1)} collective-permute-done((f32[64,2,8,1]{3,2,1,0:T(8,128)S(1)}, f32[64,2,8,1]{3,2,1,0:T(8,128)S(1)}, u32[]{:S(2)}, u32[]{:S(2)}) %collective-permute-start.14) | collective-permute-done | bytes 4128 | tf_op jit(solution)/shard_map/ppermute | solution.py:110
  341.2 3.4 concatenate.155
  344.6 2.4 fusion.274
  347.8 3.8 all-to-all-start.8
  351.6 7.5 %all-to-all-done.8 = f32[32,8,128]{2,1,0:T(8,128)S(1)} async-done(((f32[32,8,128]{2,1,0:T(8,128)}), f32[32,8,128]{2,1,0:T(8,128)S(1)}, u32[]{:S(2)}, u32[]{:S(2)}) %all-to-all-start.8) | async-done | bytes 131104 | tf_op jit(solution)/shard_map/all_to_all | solution.py:77
  359.7 3.6 all-to-all-start.9
  363.8 6.5 %all-to-all-done.9 = f32[8,8,128]{2,1,0:T(8,128)S(1)} async-done(((f32[8,8,128]{2,1,0:T(8,128)}), f32[8,8,128]{2,1,0:T(8,128)S(1)}, u32[]{:S(2)}, u32[]{:S(2)}) %all-to-all-start.9) | async-done | bytes 32800 | tf_op jit(solution)/shard_map/all_to_all | solution.py:77
  370.9 5.4 %all-to-all-start.10 = ((f32[32,8,128]{2,1,0:T(8,128)}), f32[32,8,128]{2,1,0:T(8,128)S(1)}, u32[]{:S(2)}, u32[]{:S(2)}) async-start(f32[32,8,128]{2,1,0:T(8,128)} %broadcast_in_dim.33), calls=%async_computation.10 | async-start | bytes 262144 | tf_op jit(solution)/shard_map/all_to_all | solution.py:77
  376.7 7.3 %all-to-all-done.10 = f32[32,8,128]{2,1,0:T(8,128)S(1)} async-done(((f32[32,8,128]{2,1,0:T(8,128)}), f32[32,8,128]{2,1,0:T(8,128)S(1)}, u32[]{:S(2)}, u32[]{:S(2)}) %all-to-all-start.10) | async-done | bytes 131104 | tf_op jit(solution)/shard_map/all_to_all | solution.py:77
  384.1 5.8 %cholesky.122 = f32[64,64]{1,0:T(8,128)S(1)} custom-call(f32[64,64]{1,0:T(8,128)S(1)} %fusion.55), custom_call_target="Cholesky" | custom-call | tf_op jit(solution)/shard_map/jit(cholesky)/cholesky | solution.py:135
  391.3 4.9 %custom-call.12 = f32[1,64,64]{1,2,0:T(8,128)S(1)} custom-call(f32[1,64,64]{2,1,0:T(8,128)S(1)} %select_bitcast_fusion.1), custom_call_target="InvertDiagBlocksLowerTriangular" | custom-call | tf_op jit(solution)/shard_map/jit(_solve_triangular)/triangular_solve | solution.py:136
  410.2 11.2 %all_to_all.71 = f32[32,8,128]{2,1,0:T(8,128)S(1)} all-to-all(f32[32,8,128]{2,1,0:T(8,128)S(1)} %pad_bitcast_fusion), channel_id=1, replica_groups=mesh['bx'=4,'by'=8,'bz'=8] {'bx','by'}, dimensions={0} | all-to-all | bytes 262144 | tf_op jit(solution)/shard_map/all_to_all | solution.py:77
  421.5 9.2 %all_to_all.72 = f32[8,8,128]{2,1,0:T(8,128)S(1)} all-to-all(f32[8,8,128]{2,1,0:T(8,128)S(1)} %broadcast_in_dim.35), channel_id=1, replica_groups=mesh['bx'=4,'by'=8,'bz'=8] {'bz'}, dimensions={0} | all-to-all | bytes 65536 | tf_op jit(solution)/shard_map/all_to_all | solution.py:77
  431.4 5.4 %all-to-all-start.13 = ((f32[32,8,128]{2,1,0:T(8,128)}), f32[32,8,128]{2,1,0:T(8,128)S(1)}, u32[]{:S(2)}, u32[]{:S(2)}) async-start(f32[32,8,128]{2,1,0:T(8,128)} %broadcast_in_dim.36), calls=%async_computation.13 | async-start | bytes 262144 | tf_op jit(solution)/shard_map/all_to_all | solution.py:77
  438.3 6.2 %all-to-all-done.13 = f32[32,8,128]{2,1,0:T(8,128)S(1)} async-done(((f32[32,8,128]{2,1,0:T(8,128)}), f32[32,8,128]{2,1,0:T(8,128)S(1)}, u32[]{:S(2)}, u32[]{:S(2)}) %all-to-all-start.13) | async-done | bytes 131104 | tf_op jit(solution)/shard_map/all_to_all | solution.py:77
  446.0 5.8 %cholesky.133 = f32[64,64]{1,0:T(8,128)S(1)} custom-call(f32[64,64]{1,0:T(8,128)S(1)} %fusion.53), custom_call_target="Cholesky" | custom-call | tf_op jit(solution)/shard_map/jit(cholesky)/cholesky | solution.py:135
  453.7 4.9 %custom-call.13 = f32[1,64,64]{1,2,0:T(8,128)S(1)} custom-call(f32[1,64,64]{2,1,0:T(8,128)S(1)} %get-tuple-element.5), custom_call_target="InvertDiagBlocksLowerTriangular" | custom-call | tf_op jit(solution)/shard_map/jit(_solve_triangular)/triangular_solve | solution.py:136
  (433 shorter events, 154.6 us)
Async XLA Ops:
  0.6 75.1 %copy-start = (f32[64,64]{1,0:T(8,128)S(1)}, f32[64,64]{1,0:T(8,128)}, u32[]{:S(2)}) copy-start(f32[64,64]{1,0:T(8,128)} %param.17) | copy-start | bytes 49156
  7.8 10.2 %copy-start.2 = (f32[64,2,8,128]{3,2,1,0:T(8,128)S(1)}, f32[64,2,8,128]{3,2,1,0:T(8,128)}, u32[]{:S(2)}) copy-start(f32[64,2,8,128]{3,2,1,0:T(8,128)} %param.16) | copy-start | bytes 1572868
  8.1 16.2 %copy-start.8 = (f32[70,1024]{1,0:T(8,128)}, f32[70,1024]{1,0:T(8,128)S(1)}, u32[]{:S(2)}) copy-start(f32[70,1024]{1,0:T(8,128)S(1)} %mul.446) | copy-start | bytes 860164
  9.3 35.6 %all-to-all-start = ((f32[32,8,128]{2,1,0:T(8,128)}), f32[32,8,128]{2,1,0:T(8,128)}, u32[]{:S(2)}, u32[]{:S(2)}) async-start(f32[32,8,128]{2,1,0:T(8,128)} %bitcast.2), calls=%async_computation | async-start | bytes 262144 | tf_op jit(solution)/shard_map/all_to_all | solution.py:77
  18.8 86.0 %collective-permute-start.3 = (f32[64,1,8,128]{3,2,1,0:T(8,128)}, f32[64,1,8,128]{3,2,1,0:T(8,128)}, u32[]{:S(2)}, u32[]{:S(2)}) collective-permute-start(f32[64,1,8,128]{3,2,1,0:T(8,128)} %get-tuple-element.34), channel_id=1, source_target_pairs={{0,192},{64,0},{128,64},{192,128},{1,193},{65,1},{129,65},{193,129... | collective-permute-start | bytes 786440 | tf_op jit(solution)/shard_map/ppermute | solution.py:113
  19.1 86.8 %collective-permute-start = (f32[64,1,8,128]{3,2,1,0:T(8,128)}, f32[64,1,8,128]{3,2,1,0:T(8,128)}, u32[]{:S(2)}, u32[]{:S(2)}) collective-permute-start(f32[64,1,8,128]{3,2,1,0:T(8,128)} %get-tuple-element.33), channel_id=1, source_target_pairs={{0,64},{64,128},{128,192},{192,0},{1,65},{65,129},{129,193},{193,1... | collective-permute-start | bytes 786440 | tf_op jit(solution)/shard_map/ppermute | solution.py:108
  22.8 29.6 %collective-permute-start.1 = (f32[64,2,1,128]{3,2,1,0:T(1,128)}, f32[64,2,1,128]{3,2,1,0:T(1,128)}, u32[]{:S(2)}, u32[]{:S(2)}) collective-permute-start(f32[64,2,1,128]{3,2,1,0:T(1,128)} %get-tuple-element.32), channel_id=1, source_target_pairs={{0,8},{8,16},{16,24},{24,32},{32,40},{40,48},{48,56},{56,0},{1,9},... | collective-permute-start | bytes 196616 | tf_op jit(solution)/shard_map/ppermute | solution.py:109
  24.3 17.8 %collective-permute-start.2 = (f32[64,2,8,1]{3,2,1,0:T(8,128)S(1)}, f32[64,2,8,1]{3,2,1,0:T(8,128)S(1)}, u32[]{:S(2)}, u32[]{:S(2)}) collective-permute-start(f32[64,2,8,1]{3,2,1,0:T(8,128)S(1)} %get-tuple-element.28), channel_id=1, source_target_pairs={{0,1},{1,2},{2,3},{3,4},{4,5},{5,6},{6,7},{7,0},{8,9},{9,10},{10,1... | collective-permute-start | bytes 12296 | tf_op jit(solution)/shard_map/ppermute | solution.py:110
  26.1 18.1 %collective-permute-start.5 = (f32[64,2,8,1]{3,2,1,0:T(8,128)S(1)}, f32[64,2,8,1]{3,2,1,0:T(8,128)S(1)}, u32[]{:S(2)}, u32[]{:S(2)}) collective-permute-start(f32[64,2,8,1]{3,2,1,0:T(8,128)S(1)} %get-tuple-element.27), channel_id=1, source_target_pairs={{0,7},{1,0},{2,1},{3,2},{4,3},{5,4},{6,5},{7,6},{8,15},{9,8},{10,9... | collective-permute-start | bytes 12296 | tf_op jit(solution)/shard_map/ppermute | solution.py:115
  42.1 10.2 %collective-permute-start.4 = (f32[64,2,1,128]{3,2,1,0:T(1,128)}, f32[64,2,1,128]{3,2,1,0:T(1,128)}, u32[]{:S(2)}, u32[]{:S(2)}) collective-permute-start(f32[64,2,1,128]{3,2,1,0:T(1,128)} %get-tuple-element.31), channel_id=1, source_target_pairs={{0,56},{8,0},{16,8},{24,16},{32,24},{40,32},{48,40},{56,48},{1,57}... | collective-permute-start | bytes 196616 | tf_op jit(solution)/shard_map/ppermute | solution.py:114
  46.5 13.3 %all-to-all-start.1 = ((f32[32,8,128]{2,1,0:T(8,128)}), f32[32,8,128]{2,1,0:T(8,128)}, u32[]{:S(2)}, u32[]{:S(2)}) async-start(f32[32,8,128]{2,1,0:T(8,128)} %broadcast_in_dim.26), calls=%async_computation.1 | async-start | bytes 262144 | tf_op jit(solution)/shard_map/all_to_all | solution.py:77
  122.6 21.5 %copy-start.14 = (f32[64,1,8,128]{3,2,1,0:T(8,128)}, f32[64,1,8,128]{3,2,1,0:T(8,128)S(1)}, u32[]{:S(2)}) copy-start(f32[64,1,8,128]{3,2,1,0:T(8,128)S(1)} %get-tuple-element.24) | copy-start | bytes 786436
  126.0 18.2 %collective-permute-start.6 = (f32[64,1,8,128]{3,2,1,0:T(8,128)S(1)}, f32[64,1,8,128]{3,2,1,0:T(8,128)S(1)}, u32[]{:S(2)}, u32[]{:S(2)}) collective-permute-start(f32[64,1,8,128]{3,2,1,0:T(8,128)S(1)} %get-tuple-element.23), channel_id=1, source_target_pairs={{0,64},{64,128},{128,192},{192,0},{1,65},{65,129},{129,193},{193,1... | collective-permute-start | bytes 786440 | tf_op jit(solution)/shard_map/ppermute | solution.py:108
  127.7 14.2 %collective-permute-start.8 = (f32[64,2,8,1]{3,2,1,0:T(8,128)S(1)}, f32[64,2,8,1]{3,2,1,0:T(8,128)S(1)}, u32[]{:S(2)}, u32[]{:S(2)}) collective-permute-start(f32[64,2,8,1]{3,2,1,0:T(8,128)S(1)} %get-tuple-element.18), channel_id=1, source_target_pairs={{0,1},{1,2},{2,3},{3,4},{4,5},{5,6},{6,7},{7,0},{8,9},{9,10},{10,1... | collective-permute-start | bytes 12296 | tf_op jit(solution)/shard_map/ppermute | solution.py:110
  128.4 14.7 %collective-permute-start.7 = (f32[64,2,1,128]{3,2,1,0:T(1,128)S(1)}, f32[64,2,1,128]{3,2,1,0:T(1,128)S(1)}, u32[]{:S(2)}, u32[]{:S(2)}) collective-permute-start(f32[64,2,1,128]{3,2,1,0:T(1,128)S(1)} %get-tuple-element.22), channel_id=1, source_target_pairs={{0,8},{8,16},{16,24},{24,32},{32,40},{40,48},{48,56},{56,0},{1,9},... | collective-permute-start | bytes 196616 | tf_op jit(solution)/shard_map/ppermute | solution.py:109
  151.7 11.2 %all-to-all-start.2 = ((f32[32,8,128]{2,1,0:T(8,128)}), f32[32,8,128]{2,1,0:T(8,128)S(1)}, u32[]{:S(2)}, u32[]{:S(2)}) async-start(f32[32,8,128]{2,1,0:T(8,128)} %bitcast.21), calls=%async_computation.2 | async-start | bytes 262144 | tf_op jit(solution)/shard_map/all_to_all | solution.py:77
  155.4 62.2 %copy-start.31 = (f32[10,64]{1,0:T(8,128)S(1)}, f32[10,64]{1,0:T(8,128)}, u32[]{:S(2)}) copy-start(f32[10,64]{1,0:T(8,128)} %copy-done.30) | copy-start | bytes 7684
  155.4 63.0 %copy-start.19 = (f32[3,64,64]{1,2,0:T(8,128)S(1)}, f32[3,64,64]{1,2,0:T(8,128)}, u32[]{:S(2)}) copy-start(f32[3,64,64]{1,2,0:T(8,128)} %copy-done.18) | copy-start | bytes 147460
  163.6 55.0 %copy-start.17 = (f32[3,64,64]{1,2,0:T(8,128)S(1)}, f32[3,64,64]{1,2,0:T(8,128)}, u32[]{:S(2)}) copy-start(f32[3,64,64]{1,2,0:T(8,128)} %copy-done.16) | copy-start | bytes 147460
  163.6 12.3 %all-to-all-start.3 = ((f32[8,8,128]{2,1,0:T(8,128)}), f32[8,8,128]{2,1,0:T(8,128)S(1)}, u32[]{:S(2)}, u32[]{:S(2)}) async-start(f32[8,8,128]{2,1,0:T(8,128)} %broadcast_in_dim.27), calls=%async_computation.3 | async-start | bytes 65536 | tf_op jit(solution)/shard_map/all_to_all | solution.py:77
  176.6 21.5 %all-to-all-start.4 = ((f32[32,8,128]{2,1,0:T(8,128)}), f32[32,8,128]{2,1,0:T(8,128)S(1)}, u32[]{:S(2)}, u32[]{:S(2)}) async-start(f32[32,8,128]{2,1,0:T(8,128)} %broadcast_in_dim.28), calls=%async_computation.4 | async-start | bytes 262144 | tf_op jit(solution)/shard_map/all_to_all | solution.py:77
  198.1 22.6 %copy-start.11 = (f32[7,1024]{1,0:T(8,128)S(1)}, f32[7,1024]{1,0:T(8,128)}, u32[]{:S(2)}) copy-start(f32[7,1024]{1,0:T(8,128)} %copy-done.10) | copy-start | bytes 86020
  225.7 17.5 %copy-start.15 = (f32[64,1,8,128]{3,2,1,0:T(8,128)S(1)}, f32[64,1,8,128]{3,2,1,0:T(8,128)}, u32[]{:S(2)}) copy-start(f32[64,1,8,128]{3,2,1,0:T(8,128)} %copy-done.14) | copy-start | bytes 786436
  225.7 20.9 %copy-start.32 = (f32[64,2,1,128]{3,2,1,0:T(1,128)S(1)}, f32[64,2,1,128]{3,2,1,0:T(1,128)}, u32[]{:S(2)}) copy-start(f32[64,2,1,128]{3,2,1,0:T(1,128)} %get-tuple-element.21) | copy-start | bytes 196612
  225.8 32.7 %copy-start.7 = (f32[64,2,8,127]{3,2,1,0:T(8,128)S(1)}, f32[64,2,8,127]{3,2,1,0:T(8,128)}, u32[]{:S(2)}) copy-start(f32[64,2,8,127]{3,2,1,0:T(8,128)} %get-tuple-element.15) | copy-start | bytes 1560580
  239.9 10.5 %all-to-all-start.6 = ((f32[8,16,128]{2,1,0:T(8,128)}), f32[8,16,128]{2,1,0:T(8,128)S(1)}, u32[]{:S(2)}, u32[]{:S(2)}) async-start(f32[8,16,128]{2,1,0:T(8,128)} %broadcast_in_dim.30), calls=%async_computation.6 | async-start | bytes 131072 | tf_op jit(solution)/shard_map/all_to_all | solution.py:77
  243.3 17.7 %collective-permute-start.9 = (f32[64,1,8,128]{3,2,1,0:T(8,128)S(1)}, f32[64,1,8,128]{3,2,1,0:T(8,128)}, u32[]{:S(2)}, u32[]{:S(2)}) collective-permute-start(f32[64,1,8,128]{3,2,1,0:T(8,128)S(1)} %copy-done.15), channel_id=1, source_target_pairs={{0,192},{64,0},{128,64},{192,128},{1,193},{65,1},{129,65},{193,129... | collective-permute-start | bytes 786440 | tf_op jit(solution)/shard_map/ppermute | solution.py:113
  243.8 14.7 %collective-permute-start.11 = (f32[64,2,8,1]{3,2,1,0:T(8,128)}, f32[64,2,8,1]{3,2,1,0:T(8,128)S(1)}, u32[]{:S(2)}, u32[]{:S(2)}) collective-permute-start(f32[64,2,8,1]{3,2,1,0:T(8,128)} %get-tuple-element.17), channel_id=1, source_target_pairs={{0,7},{1,0},{2,1},{3,2},{4,3},{5,4},{6,5},{7,6},{8,15},{9,8},{10,9... | collective-permute-start | bytes 12296 | tf_op jit(solution)/shard_map/ppermute | solution.py:115
  246.6 12.3 %collective-permute-start.10 = (f32[64,2,1,128]{3,2,1,0:T(1,128)S(1)}, f32[64,2,1,128]{3,2,1,0:T(1,128)S(1)}, u32[]{:S(2)}, u32[]{:S(2)}) collective-permute-start(f32[64,2,1,128]{3,2,1,0:T(1,128)S(1)} %copy-done.32), channel_id=1, source_target_pairs={{0,56},{8,0},{16,8},{24,16},{32,24},{40,32},{48,40},{56,48},{1,57}... | collective-permute-start | bytes 196616 | tf_op jit(solution)/shard_map/ppermute | solution.py:114
  251.1 14.4 %all-to-all-start.7 = ((f32[32,16,128]{2,1,0:T(8,128)}), f32[32,16,128]{2,1,0:T(8,128)S(1)}, u32[]{:S(2)}, u32[]{:S(2)}) async-start(f32[32,16,128]{2,1,0:T(8,128)} %broadcast_in_dim.31), calls=%async_computation.7 | async-start | bytes 524288 | tf_op jit(solution)/shard_map/all_to_all | solution.py:77
  262.0 14.1 %copy-start.43 = (f32[10,10]{1,0:T(8,128)S(1)}, f32[10,10]{1,0:T(8,128)}, u32[]{:S(2)}) copy-start(f32[10,10]{1,0:T(8,128)} %constant.194.clone) | copy-start | bytes 1204
  262.0 14.4 %copy-start.42 = (f32[10,10]{1,0:T(8,128)S(1)}, f32[10,10]{1,0:T(8,128)}, u32[]{:S(2)}) copy-start(f32[10,10]{1,0:T(8,128)} %constant.195.clone) | copy-start | bytes 1204
  262.0 16.6 %copy-start.41 = (f32[10,10]{1,0:T(8,128)S(1)}, f32[10,10]{1,0:T(8,128)}, u32[]{:S(2)}) copy-start(f32[10,10]{1,0:T(8,128)} %constant.196.clone) | copy-start | bytes 1204
  262.0 18.1 %copy-start.40 = (f32[10,10]{1,0:T(8,128)S(1)}, f32[10,10]{1,0:T(8,128)}, u32[]{:S(2)}) copy-start(f32[10,10]{1,0:T(8,128)} %constant.197.clone) | copy-start | bytes 1204
  263.0 18.6 %copy-start.39 = (f32[10,10]{1,0:T(8,128)S(1)}, f32[10,10]{1,0:T(8,128)}, u32[]{:S(2)}) copy-start(f32[10,10]{1,0:T(8,128)} %constant.198.clone) | copy-start | bytes 1204
  263.0 20.1 %copy-start.38 = (f32[10,10]{1,0:T(8,128)S(1)}, f32[10,10]{1,0:T(8,128)}, u32[]{:S(2)}) copy-start(f32[10,10]{1,0:T(8,128)} %constant.199.clone) | copy-start | bytes 1204
  290.3 15.6 %copy-start.4 = (f32[8,8,16,128]{3,1,2,0:T(8,128)S(1)}, f32[8,8,16,128]{3,1,2,0:T(8,128)}, u32[]{:S(2)}) copy-start(f32[8,8,16,128]{3,1,2,0:T(8,128)} %copy.353) | copy-start | bytes 1572868
  290.3 15.6 %copy-start.5 = (f32[8,8,16,128]{3,1,2,0:T(8,128)S(1)}, f32[8,8,16,128]{3,1,2,0:T(8,128)}, u32[]{:S(2)}) copy-start(f32[8,8,16,128]{3,1,2,0:T(8,128)} %copy.354) | copy-start | bytes 1572868
  290.3 15.6 %copy-start.6 = (f32[8,8,16,128]{3,1,2,0:T(8,128)S(1)}, f32[8,8,16,128]{3,1,2,0:T(8,128)}, u32[]{:S(2)}) copy-start(f32[8,8,16,128]{3,1,2,0:T(8,128)} %copy.355) | copy-start | bytes 1572868
  322.0 18.2 %collective-permute-start.12 = (f32[64,1,8,128]{3,2,1,0:T(8,128)S(1)}, f32[64,1,8,128]{3,2,1,0:T(8,128)S(1)}, u32[]{:S(2)}, u32[]{:S(2)}) collective-permute-start(f32[64,1,8,128]{3,2,1,0:T(8,128)S(1)} %get-tuple-element.13), channel_id=1, source_target_pairs={{0,64},{64,128},{128,192},{192,0},{1,65},{65,129},{129,193},{193,1... | collective-permute-start | bytes 786440 | tf_op jit(solution)/shard_map/ppermute | solution.py:108
  323.9 14.0 %collective-permute-start.14 = (f32[64,2,8,1]{3,2,1,0:T(8,128)S(1)}, f32[64,2,8,1]{3,2,1,0:T(8,128)S(1)}, u32[]{:S(2)}, u32[]{:S(2)}) collective-permute-start(f32[64,2,8,1]{3,2,1,0:T(8,128)S(1)} %slice.687), channel_id=1, source_target_pairs={{0,1},{1,2},{2,3},{3,4},{4,5},{5,6},{6,7},{7,0},{8,9},{9,10},{10,1... | collective-permute-start | bytes 12296 | tf_op jit(solution)/shard_map/ppermute | solution.py:110
  324.5 14.7 %collective-permute-start.13 = (f32[64,2,1,128]{3,2,1,0:T(1,128)S(1)}, f32[64,2,1,128]{3,2,1,0:T(1,128)S(1)}, u32[]{:S(2)}, u32[]{:S(2)}) collective-permute-start(f32[64,2,1,128]{3,2,1,0:T(1,128)S(1)} %slice.685), channel_id=1, source_target_pairs={{0,8},{8,16},{16,24},{24,32},{32,40},{40,48},{48,56},{56,0},{1,9},... | collective-permute-start | bytes 196616 | tf_op jit(solution)/shard_map/ppermute | solution.py:109
  347.8 11.3 %all-to-all-start.8 = ((f32[32,8,128]{2,1,0:T(8,128)}), f32[32,8,128]{2,1,0:T(8,128)S(1)}, u32[]{:S(2)}, u32[]{:S(2)}) async-start(f32[32,8,128]{2,1,0:T(8,128)} %bitcast.64), calls=%async_computation.8 | async-start | bytes 262144 | tf_op jit(solution)/shard_map/all_to_all | solution.py:77
  359.7 10.5 %all-to-all-start.9 = ((f32[8,8,128]{2,1,0:T(8,128)}), f32[8,8,128]{2,1,0:T(8,128)S(1)}, u32[]{:S(2)}, u32[]{:S(2)}) async-start(f32[8,8,128]{2,1,0:T(8,128)} %broadcast_in_dim.32), calls=%async_computation.9 | async-start | bytes 65536 | tf_op jit(solution)/shard_map/all_to_all | solution.py:77
  370.9 13.1 %all-to-all-start.10 = ((f32[32,8,128]{2,1,0:T(8,128)}), f32[32,8,128]{2,1,0:T(8,128)S(1)}, u32[]{:S(2)}, u32[]{:S(2)}) async-start(f32[32,8,128]{2,1,0:T(8,128)} %broadcast_in_dim.33), calls=%async_computation.10 | async-start | bytes 262144 | tf_op jit(solution)/shard_map/all_to_all | solution.py:77
  410.0 34.6 %copy-start.37 = (f32[10,10]{1,0:T(8,128)S(1)}, f32[10,10]{1,0:T(8,128)}, u32[]{:S(2)}) copy-start(f32[10,10]{1,0:T(8,128)} %constant.193.clone) | copy-start | bytes 1204
  431.4 13.0 %all-to-all-start.13 = ((f32[32,8,128]{2,1,0:T(8,128)}), f32[32,8,128]{2,1,0:T(8,128)S(1)}, u32[]{:S(2)}, u32[]{:S(2)}) async-start(f32[32,8,128]{2,1,0:T(8,128)} %broadcast_in_dim.36), calls=%async_computation.13 | async-start | bytes 262144 | tf_op jit(solution)/shard_map/all_to_all | solution.py:77
  436.8 23.2 %copy-start.1 = (f32[64,64]{1,0:T(8,128)S(1)}, f32[64,64]{1,0:T(8,128)}, u32[]{:S(2)}) copy-start(f32[64,64]{1,0:T(8,128)} %param.17) | copy-start | bytes 49156
  (22 other events, 119.4 us)
